TPU v7x, 256 devices: a whole 4x4x8 slice. The times are simulated.
256 devices in a mesh: row: 16 (over x, z_lo, core), col: 16 (over y, z_hi).
Axes of the slice: x: 4, y: 4, z: 8 (z_hi: 4, z_lo: 2; z = z_hi * 2 + z_lo), core: 2. Of those that a mesh axis runs over, the one named last changes fastest.
Arguments:
- ancestor_inverse: bfloat16 [32768, 32768], P('row', 'col'), may hold values from -0.03125 to 0.03125
- panel: bfloat16 [32768, 512], P(('row', 'col')), may hold values from -0.75 to 0.75
- structure: int32 [2, 128], replicated, may hold values 0 or 1
- diag_inverse: float32 [2, 256, 256], replicated, may hold values from -6 to 6
Outputs:
- upper: bfloat16 [32768, 512], P(('row', 'col'))
- diagonal: float32 [2, 256, 256], replicated
All inputs are finite; a program needn't handle non-finite values.
Results may differ from a plain program's by a relative error of at most 0.0014.
Values may be sent and summed in bfloat16 or wider, within the bound.
A program may use at most 64 MiB of HBM per device.

v0:
```python
import jax
import jax.numpy as jnp
from jax import lax
from jax.sharding import PartitionSpec as P


def from_root(block, axis, source):
    block = jnp.where(lax.axis_index(axis) == source, block, jnp.zeros_like(block))
    return lax.psum(block, axis)


def row_keep(begin_row, length, structure, blk_width):
    blocks_all = structure.shape[1]
    indices = begin_row + jnp.arange(length, dtype=jnp.int32)
    owners = indices // blk_width
    onehot = (owners[:, None] == jnp.arange(blocks_all, dtype=jnp.int32)[None, :]).astype(
        jnp.float32
    )
    keeps = jnp.dot(onehot, structure.T.astype(jnp.float32), preferred_element_type=jnp.float32)
    return jnp.repeat(keeps, blk_width, axis=1)


def diag_part(lower, upper_rows, blk_width):
    snodes = upper_rows.shape[1] // blk_width
    lower_f = lower.astype(jnp.float32).reshape(lower.shape[0], snodes, blk_width)
    upper_f = upper_rows.reshape(upper_rows.shape[0], snodes, blk_width)
    return jnp.einsum("mkw,mkv->kwv", lower_f, upper_f, precision=lax.Precision.HIGHEST)


def local(ancestor_inverse, panel, structure, diag_inverse):
    blk_width = diag_inverse.shape[1]
    row_count = lax.axis_size("row")
    col_count = lax.axis_size("col")
    row_index = lax.axis_index("row")
    col_index = lax.axis_index("col")
    piece_rows = panel.shape[0]
    begin_own = (row_index * col_count + col_index) * piece_rows
    keep_own = row_keep(begin_own, piece_rows, structure, blk_width)
    masked = panel * keep_own.astype(jnp.bfloat16)
    row_block = lax.all_gather(masked, "col", axis=0, tiled=True)
    ratio = col_count // row_count
    root_row = col_index // ratio
    col_block = from_root(row_block, "row", root_row)
    partial_rows = -jnp.dot(ancestor_inverse, col_block, preferred_element_type=jnp.float32)
    full_rows = lax.psum(partial_rows, "col")
    own_rows = lax.dynamic_slice_in_dim(full_rows, col_index * piece_rows, piece_rows, 0)
    diag_sum = lax.psum(diag_part(masked, own_rows, blk_width), ("row", "col"))
    upper = (own_rows * keep_own).astype(jnp.bfloat16)
    diagonal = diag_inverse - diag_sum
    return (upper, diagonal)


def solution(mesh):
    return jax.shard_map(
        local,
        mesh=mesh,
        in_specs=(P("row", "col"), P(("row", "col"), None), P(), P()),
        out_specs=(P(("row", "col"), None), P()),
        check_vma=False,
    )
```

profile of v0, /device:TPU:2, one launch (start us, length us, event | category | flops | bytes accessed | tf_op | source)
XLA Modules:
  0.0 704.9 jit_solution(14977769221147062847)
XLA Ops:
  7.2 0.0 all-gather.2.cloned.1.call-start
  7.2 1.0 copy.8
  8.3 0.9 fusion.2
  9.1 0.7 fusion.1
  9.8 0.0 all-gather.2.cloned.1.call-update
  9.9 0.0 all-reduce.4.cloned.1.call-start
  9.9 66.3 %all-gather.2.cloned.1.call-done = bf16[2048,512]{0,1:T(8,128)(2,1)} async-done(((bf16[128,512]{0,1:T(8,128)(2,1)}), bf16[2048,512]{0,1:T(8,128)(2,1)}) %all-gather.2.cloned.1.call-update) | async-done | bytes 2097168 | tf_op jit(solution)/shard_map/all_gather | solution.py:40
  76.2 1.5 broadcast_select_fusion
  77.7 0.0 all-reduce.4.cloned.1.call-update
  77.7 0.0 all-reduce.6.cloned.1.call-start
  77.8 122.7 %all-reduce.4.cloned.1.call-done = bf16[2048,512]{0,1:T(8,128)(2,1)} async-done(((bf16[2048,512]{0,1:T(8,128)(2,1)}), bf16[2048,512]{0,1:T(8,128)(2,1)}) %all-reduce.4.cloned.1.call-update) | async-done | bytes 2097168 | tf_op jit(solution)/shard_map/psum | solution.py:9
  200.5 10.5 %negate_bitcast_fusion = f32[2048,512]{0,1:T(8,128)} fusion(bf16[2048,512]{0,1:T(8,128)(2,1)} %all-reduce.4.cloned.1.call-done, bf16[2048,2048]{1,0:T(8,128)(2,1)} %param.4), kind=kOutput, calls=%fused_computation | convolution fusion | flops 4296015872 | bytes 14680064 | tf_op jit(solution)/shard_map/dot_general | solution.py:44
  211.0 0.0 copy-start
  211.0 0.0 copy-start.1
  211.0 0.0 all-reduce.6.cloned.1.call-update
  211.0 0.0 all-reduce.8.cloned.1.call-start
  211.1 225.6 %all-reduce.6.cloned.1.call-done = f32[2048,512]{0,1:T(8,128)} async-done(((f32[2048,512]{0,1:T(8,128)}), f32[2048,512]{0,1:T(8,128)}) %all-reduce.6.cloned.1.call-update) | async-done | bytes 4194320 | tf_op jit(solution)/shard_map/psum | solution.py:45
  436.7 1.0 fusion
  437.7 0.0 copy-done
  437.7 1.2 fusion.5
  438.9 0.0 all-reduce.8.cloned.1.call-update
  438.9 0.8 copy.10
  439.7 256.8 %all-reduce.8.cloned.1.call-done = f32[2,256,256]{2,1,0:T(8,128)} async-done(((f32[2,256,256]{2,1,0:T(8,128)}), f32[2,256,256]{2,1,0:T(8,128)}) %all-reduce.8.cloned.1.call-update) | async-done | bytes 524304 | tf_op jit(solution)/shard_map/psum | solution.py:47
  696.4 0.0 copy-done.1
  696.4 1.9 sub.12
  (1 shorter events, 0.0 us)
Async XLA Ops:
  7.2 69.0 %all-gather.2.cloned.1.call-start = ((), (), s32[]{:S(2)}) async-start(), calls=%async_computation | async-start | bytes 2228224 | tf_op jit(solution)/shard_map/all_gather | solution.py:40
  9.9 190.6 %all-reduce.4.cloned.1.call-start = ((), (), s32[]{:S(2)}) async-start(), calls=%async_computation.1 | async-start | bytes 4194304 | tf_op jit(solution)/shard_map/psum | solution.py:9
  77.7 359.0 %all-reduce.6.cloned.1.call-start = ((), (), s32[]{:S(2)}) async-start(), calls=%async_computation.2 | async-start | bytes 8388608 | tf_op jit(solution)/shard_map/psum | solution.py:45
  211.0 226.7 %copy-start = (bf16[128,512]{0,1:T(8,128)(2,1)S(1)}, bf16[128,512]{0,1:T(8,128)(2,1)}, u32[]{:S(2)}) copy-start(bf16[128,512]{0,1:T(8,128)(2,1)} %fusion.1) | copy-start | bytes 393220
  211.0 485.5 %copy-start.1 = (f32[2,256,256]{2,1,0:T(8,128)S(1)}, f32[2,256,256]{2,1,0:T(8,128)}, u32[]{:S(2)}) copy-start(f32[2,256,256]{2,1,0:T(8,128)} %param.7) | copy-start | bytes 1572868
  211.0 485.4 %all-reduce.8.cloned.1.call-start = ((), (), s32[]{:S(2)}) async-start(), calls=%async_computation.3 | async-start | bytes 1048576 | tf_op jit(solution)/shard_map/psum | solution.py:47
Sparse Core Ops, SparseCore 0:
  10.9 65.2 all-gather.1
  78.9 121.5 all-reduce.3
  211.1 225.5 all-reduce.5
  442.6 253.8 all-reduce.7
where the time goes:
time: 705 us
  waiting for transfers between devices  671 us (95%)
  between operations  13.8 us (2%)
  matrix products  12.6 us (2%)
    psum x1, waiting for transfers between devices, local(): diag_sum = lax.psum(diag_part(masked, own_rows, blk_width), ('row', 'col'))  257 us
    psum x1, waiting for transfers between devices, local(): full_rows = lax.psum(partial_rows, 'col')  226 us
    psum x1, waiting for transfers between devices, from_root(): return lax.psum(block, axis)  123 us
    all_gather x1, waiting for transfers between devices, local(): row_block = lax.all_gather(masked, 'col', axis=0, tiled=True)  66.3 us
  transfers between devices with their start and end apart: 4, of which 4 were waited for; matrix products, arithmetic and copies ran while one was open for 0% of the time, Pallas kernels for 0%

commit v1 on v0

--- a/solution.py
+++ b/solution.py
@@ -44,7 +44,7 @@
     partial_rows = -jnp.dot(ancestor_inverse, col_block, preferred_element_type=jnp.float32)
     full_rows = lax.psum(partial_rows, "col")
     own_rows = lax.dynamic_slice_in_dim(full_rows, col_index * piece_rows, piece_rows, 0)
-    diag_sum = lax.psum(diag_part(masked, own_rows, blk_width), ("row", "col"))
+    diag_sum = lax.psum(lax.psum(diag_part(masked, own_rows, blk_width), "row"), "col")
     upper = (own_rows * keep_own).astype(jnp.bfloat16)
     diagonal = diag_inverse - diag_sum
     return (upper, diagonal)

time: 705 us -> 741 us (1.051)
  waiting for transfers between devices: 671 us -> 708 us
    psum x1 -> x2, waiting for transfers between devices: 257 us -> 293 us  [the longest x1 176 us: local(): lax.psum(lax.psum(diag_part(masked, own_rows, blk_width), 'row'), 'col')]
  transfers between devices with their start and end apart: 4 -> 5, of which waited for: 4 -> 5; matrix products, arithmetic and copies ran while one was open for 0% -> 0% of each run, Pallas kernels for 0% -> 0%
where the time goes in v1:
time: 741 us
  waiting for transfers between devices  708 us (96%)
  between operations  13.8 us (2%)
  matrix products  12.6 us (2%)
    psum x1, waiting for transfers between devices, local(): full_rows = lax.psum(partial_rows, 'col')  226 us
    psum x1, waiting for transfers between devices, local(): lax.psum(lax.psum(diag_part(masked, own_rows, blk_width), 'row'), 'col')  176 us
    psum x1, waiting for transfers between devices, from_root(): return lax.psum(block, axis)  123 us
    psum x1, waiting for transfers between devices, local(): lax.psum(diag_part(masked, own_rows, blk_width), 'row')  117 us
    all_gather x1, waiting for transfers between devices, local(): row_block = lax.all_gather(masked, 'col', axis=0, tiled=True)  66.3 us
  transfers between devices with their start and end apart: 5, of which 5 were waited for; matrix products, arithmetic and copies ran while one was open for 0% of the time, Pallas kernels for 0%

profile of v1, /device:TPU:2, one launch (start us, length us, event | category | flops | bytes accessed | tf_op | source)
XLA Modules:
  0.0 741.0 jit_solution(13015117990419252098)
XLA Ops:
  7.2 0.0 all-gather.2.cloned.1.call-start
  7.2 1.0 copy.8
  8.3 0.9 fusion.2
  9.1 0.7 fusion.1
  9.8 0.0 all-gather.2.cloned.1.call-update
  9.9 0.0 all-reduce.5.cloned.1.call-start
  9.9 66.3 %all-gather.2.cloned.1.call-done = bf16[2048,512]{0,1:T(8,128)(2,1)} async-done(((bf16[128,512]{0,1:T(8,128)(2,1)}), bf16[2048,512]{0,1:T(8,128)(2,1)}) %all-gather.2.cloned.1.call-update) | async-done | bytes 2097168 | tf_op jit(solution)/shard_map/all_gather | solution.py:40
  76.2 1.5 broadcast_select_fusion
  77.7 0.0 all-reduce.5.cloned.1.call-update
  77.7 0.0 all-reduce.7.cloned.1.call-start
  77.8 122.7 %all-reduce.5.cloned.1.call-done = bf16[2048,512]{0,1:T(8,128)(2,1)} async-done(((bf16[2048,512]{0,1:T(8,128)(2,1)}), bf16[2048,512]{0,1:T(8,128)(2,1)}) %all-reduce.5.cloned.1.call-update) | async-done | bytes 2097168 | tf_op jit(solution)/shard_map/psum | solution.py:9
  200.5 10.5 %negate_bitcast_fusion = f32[2048,512]{0,1:T(8,128)} fusion(bf16[2048,512]{0,1:T(8,128)(2,1)} %all-reduce.5.cloned.1.call-done, bf16[2048,2048]{1,0:T(8,128)(2,1)} %param.4), kind=kOutput, calls=%fused_computation | convolution fusion | flops 4296015872 | bytes 14680064 | tf_op jit(solution)/shard_map/dot_general | solution.py:44
  211.0 0.0 copy-start
  211.0 0.0 copy-start.1
  211.0 0.0 all-reduce.7.cloned.1.call-update
  211.0 0.0 all-reduce.9.cloned.1.call-start
  211.1 225.6 %all-reduce.7.cloned.1.call-done = f32[2048,512]{0,1:T(8,128)} async-done(((f32[2048,512]{0,1:T(8,128)}), f32[2048,512]{0,1:T(8,128)}) %all-reduce.7.cloned.1.call-update) | async-done | bytes 4194320 | tf_op jit(solution)/shard_map/psum | solution.py:45
  436.7 1.0 fusion
  437.7 0.0 copy-done
  437.7 1.2 fusion.5
  438.9 0.0 all-reduce.9.cloned.1.call-update
  438.9 0.0 all-reduce.11.cloned.1.call-start
  438.9 117.3 %all-reduce.9.cloned.1.call-done = f32[2,256,256]{2,1,0:T(8,128)} async-done(((f32[2,256,256]{2,1,0:T(8,128)}), f32[2,256,256]{2,1,0:T(8,128)}) %all-reduce.9.cloned.1.call-update) | async-done | bytes 524304 | tf_op jit(solution)/shard_map/psum | solution.py:47
  556.3 0.0 all-reduce.11.cloned.1.call-update
  556.3 0.8 copy.10
  557.1 175.5 %all-reduce.11.cloned.1.call-done = f32[2,256,256]{2,1,0:T(8,128)} async-done(((f32[2,256,256]{2,1,0:T(8,128)}), f32[2,256,256]{2,1,0:T(8,128)}) %all-reduce.11.cloned.1.call-update) | async-done | bytes 524304 | tf_op jit(solution)/shard_map/psum | solution.py:47
  732.6 0.0 copy-done.1
  732.6 1.9 sub.12
  (1 shorter events, 0.0 us)
Async XLA Ops:
  7.2 69.0 %all-gather.2.cloned.1.call-start = ((), (), s32[]{:S(2)}) async-start(), calls=%async_computation | async-start | bytes 2228224 | tf_op jit(solution)/shard_map/all_gather | solution.py:40
  9.9 190.6 %all-reduce.5.cloned.1.call-start = ((), (), s32[]{:S(2)}) async-start(), calls=%async_computation.1 | async-start | bytes 4194304 | tf_op jit(solution)/shard_map/psum | solution.py:9
  77.7 359.0 %all-reduce.7.cloned.1.call-start = ((), (), s32[]{:S(2)}) async-start(), calls=%async_computation.2 | async-start | bytes 8388608 | tf_op jit(solution)/shard_map/psum | solution.py:45
  211.0 226.7 %copy-start = (bf16[128,512]{0,1:T(8,128)(2,1)S(1)}, bf16[128,512]{0,1:T(8,128)(2,1)}, u32[]{:S(2)}) copy-start(bf16[128,512]{0,1:T(8,128)(2,1)} %fusion.1) | copy-start | bytes 393220
  211.0 521.6 %copy-start.1 = (f32[2,256,256]{2,1,0:T(8,128)S(1)}, f32[2,256,256]{2,1,0:T(8,128)}, u32[]{:S(2)}) copy-start(f32[2,256,256]{2,1,0:T(8,128)} %param.7) | copy-start | bytes 1572868
  211.0 345.3 %all-reduce.9.cloned.1.call-start = ((), (), s32[]{:S(2)}) async-start(), calls=%async_computation.3 | async-start | bytes 1048576 | tf_op jit(solution)/shard_map/psum | solution.py:47
  438.9 293.7 %all-reduce.11.cloned.1.call-start = ((), (), s32[]{:S(2)}) async-start(), calls=%async_computation.4 | async-start | bytes 1048576 | tf_op jit(solution)/shard_map/psum | solution.py:47
Sparse Core Ops, SparseCore 0:
  10.9 65.2 all-gather.1
  78.9 121.5 all-reduce.4
  211.1 225.5 all-reduce.6
  439.7 116.5 all-reduce.8
  558.8 173.7 all-reduce.10
